TPU v7x, 512 devices: a whole 4x4x16 slice. The times are simulated.
512 devices in a mesh: dp: 32 (over z, y_lo), tensor: 16 (over y_hi, x, core).
Axes of the slice: x: 4, y: 4 (y_hi: 2, y_lo: 2; y = y_hi * 2 + y_lo), z: 16, core: 2. Of those that a mesh axis runs over, the one named last changes fastest.
Arguments:
- activations: bfloat16 [32768, 8192], P('dp', 'tensor'), may hold values from -6 to 6
- out_grads: bfloat16 [32768, 8192], P('dp', 'tensor'), may hold values from -6 to 6
- proj_in: bfloat16 [8192, 64], P('tensor'), may hold values from -0.0625 to 0.0625
- proj_out: bfloat16 [8192, 64], P('tensor'), may hold values from -0.0625 to 0.0625
- segment_ids: int32 [32, 1024], P('dp'), may hold values from 0 to 23, never falling along the last dimension, each value on 1 to 80 neighbouring positions
- train_logs: bfloat16 [131072, 4096], P('dp', 'tensor'), may hold values from -6 to 6
- doc_ids: int32 [131072], P(('dp', 'tensor')), may hold values from 0 to 255
Outputs:
- scores: float32 [768, 131072], P(None, ('dp', 'tensor'))
- doc_influence: float32 [768, 256], replicated
Inputs may be any that keep to these rules, and one draw needn't show every extreme that they name: `segment_ids`: in each row the example numbers never fall; each of the 24 examples has 1 to 80 tokens, and one has exactly 80.
All inputs are finite; a program needn't handle non-finite values.
Results may differ from a plain program's by a relative error of at most 0.0052.
Values may be sent and summed in bfloat16 or wider, within the bound.
No kernel may reach another device: no remote copies, remote signals or barrier semaphores. Data moves between devices by JAX's collectives and lax.ppermute only.
A program may use at most 64 MiB of HBM per device.

v0:
```python
import math
import jax
import jax.numpy as jnp
from jax import lax
from jax.sharding import PartitionSpec as P

EX_DEV = 24
DOCS = 256


def per_device(activations, out_grads, proj_in, proj_out, segment_ids, train_logs, doc_ids):
    width_parts = lax.axis_size("tensor")
    position = lax.axis_index("tensor")
    tok_rows = activations.shape[0]
    rank = proj_in.shape[1]
    partial_value = jnp.concatenate(
        [
            jnp.dot(activations, proj_in, preferred_element_type=jnp.float32),
            jnp.dot(out_grads, proj_out, preferred_element_type=jnp.float32),
        ],
        axis=1,
    )
    seg_row = segment_ids[0]
    labels = jnp.arange(EX_DEV, dtype=jnp.int32)
    counts = jnp.sum((seg_row[:, None] == labels[None, :]).astype(jnp.float32), axis=0)
    block_rank = rank // width_parts
    summed = lax.psum(partial_value, "tensor").astype(jnp.bfloat16)
    in_proj = summed[:, :rank]
    out_proj = summed[:, rank:]
    own_out = lax.dynamic_slice_in_dim(out_proj, position * block_rank, block_rank, 1)
    member = (seg_row[:, None] == labels[None, :]).astype(jnp.bfloat16)
    masked = (member[:, :, None] * own_out[:, None, :]).reshape(tok_rows, EX_DEV * block_rank)
    log_sums = jnp.einsum("ta,tj->aj", masked, in_proj, preferred_element_type=jnp.float32)
    log_sums = log_sums.reshape(EX_DEV, block_rank * rank)
    query_block = (log_sums / counts[:, None]).astype(jnp.bfloat16)
    train_full = lax.all_to_all(train_logs, "tensor", split_axis=0, concat_axis=1, tiled=True)
    local_rows = train_full.shape[0]
    wide_block = lax.all_gather(query_block, "tensor", axis=1, tiled=True)
    rows = lax.dot_general(
        lax.all_gather(wide_block, "dp", axis=0, tiled=True),
        train_full,
        (((1,), (1,)), ((), ())),
        preferred_element_type=jnp.float32,
    )
    scores = rows * 0.125
    doc_labels = jnp.arange(DOCS, dtype=jnp.int32)
    doc_hot = (doc_ids[:, None] == doc_labels[None, :]).astype(jnp.float32)
    doc_part = jnp.dot(scores, doc_hot, precision=lax.Precision.HIGHEST)
    total_rows = local_rows * lax.axis_size("tensor") * lax.axis_size("dp")
    doc_total = lax.psum(doc_part, ("dp", "tensor"))
    doc_influence = doc_total / math.sqrt(total_rows / DOCS)
    return (scores, doc_influence)


def solution(mesh):
    placed = (
        P("dp", "tensor"),
        P("dp", "tensor"),
        P("tensor", None),
        P("tensor", None),
        P("dp", None),
        P("dp", "tensor"),
        P(("dp", "tensor")),
    )
    return jax.shard_map(
        per_device,
        mesh=mesh,
        in_specs=placed,
        out_specs=(P(None, ("dp", "tensor")), P()),
        check_vma=False,
    )
```

profile of v0, /device:TPU:2, one launch (start us, length us, event | category | flops | bytes accessed | tf_op | source)
XLA Modules:
  0.0 761.5 jit_solution(6124716450737580398)
XLA Ops:
  7.2 0.0 copy-start
  7.2 0.0 all-gather.2.cloned.1.call-start
  7.2 0.9 convert_reduce_fusion
  8.1 0.7 fusion.4
  8.8 1.3 fusion.5
  10.1 1.7 fusion.6
  11.8 0.1 pad_maximum_fusion
  11.8 70.0 %all-reduce.4 = bf16[1024,128]{0,1:T(8,128)(2,1)S(1)} all-reduce(f32[1024,128]{0,1:T(8,128)S(1)} %pad_maximum_fusion), channel_id=1, replica_groups=mesh['dp'=32,'tensor'=16] {'tensor'}, use_global_device_ids=true, to_apply=%region_0.0 | all-reduce | flops 131072 | bytes 786432 | tf_op jit(solution)/shard_map/psum | solution.py:27
  81.9 0.1 broadcast_multiply_fusion.1
  82.0 0.1 mul.30
  82.0 0.2 fusion.1
  82.2 0.1 reshape.42
  82.3 0.1 divide_convert_fusion
  82.4 27.0 %all_gather.6 = bf16[24,4096]{1,0:T(8,128)(2,1)} all-gather(bf16[24,256]{1,0:T(8,128)(2,1)S(1)} %divide_convert_fusion), channel_id=1, replica_groups=mesh['dp'=32,'tensor'=16] {'tensor'}, dimensions={1}, use_global_device_ids=true | all-gather | bytes 208896 | tf_op jit(solution)/shard_map/all_gather | solution.py:38
  109.4 0.0 all-gather.2.cloned.1.call-update
  109.4 0.0 all-reduce.3.cloned.1.call-start
  109.4 34.0 %all_to_all.19 = bf16[16,256,256]{2,1,0:T(8,128)(2,1)S(1)} all-to-all(bf16[16,256,256]{2,1,0:T(8,128)(2,1)} %bitcast.15), channel_id=1, replica_groups=mesh['dp'=32,'tensor'=16] {'tensor'}, dimensions={0} | all-to-all | bytes 4194304 | tf_op jit(solution)/shard_map/all_to_all | solution.py:36
  143.5 2.4 copy.12
  145.9 133.8 %all-gather.2.cloned.1.call-done = bf16[768,4096]{1,0:T(8,128)(2,1)} async-done(((bf16[24,4096]{1,0:T(8,128)(2,1)}), bf16[768,4096]{1,0:T(8,128)(2,1)}) %all-gather.2.cloned.1.call-update) | async-done | bytes 6291472 | tf_op jit(solution)/shard_map/all_gather | solution.py:40
  279.7 5.2 convolution_multiply_fusion
  284.9 1.5 fusion
  286.4 0.0 all-reduce.3.cloned.1.call-update
  286.4 466.2 %all-reduce.3.cloned.1.call-done = f32[768,256]{1,0:T(8,128)} async-done(((f32[768,256]{1,0:T(8,128)}), f32[768,256]{1,0:T(8,128)}) %all-reduce.3.cloned.1.call-update) | async-done | bytes 786448 | tf_op jit(solution)/shard_map/psum | solution.py:50
  752.6 2.1 broadcast_multiply_fusion
  (7 shorter events, 0.0 us)
Async XLA Ops:
  7.2 1.7 copy-start
  7.2 272.5 %all-gather.2.cloned.1.call-start = ((), (), s32[]{:S(2)}) async-start(), calls=%async_computation.1 | async-start | bytes 6488064 | tf_op jit(solution)/shard_map/all_gather | solution.py:40
  109.4 643.2 %all-reduce.3.cloned.1.call-start = ((), (), s32[]{:S(2)}) async-start(), calls=%async_computation.2 | async-start | bytes 1572864 | tf_op jit(solution)/shard_map/psum | solution.py:50
  279.7 5.2 copy-start.2
  284.9 469.8 %copy-start.1 = (f32[768,256]{1,0:T(8,128)}, f32[768,256]{1,0:T(8,128)S(1)}, u32[]{:S(2)}) copy-start(f32[768,256]{1,0:T(8,128)S(1)} %convolution_multiply_fusion) | copy-start | bytes 2359300
Sparse Core Ops, SparseCore 0:
  109.5 170.1 all-gather.1
  286.5 466.0 all-reduce.2
where the time goes:
time: 762 us
  waiting for transfers between devices  600 us (79%)
  blocking collectives  131 us (17%)
  between operations  14.1 us (2%)
  matrix products  9.8 us (1%)
    psum x1, waiting for transfers between devices, per_device(): doc_total = lax.psum(doc_part, ('dp', 'tensor'))  466 us
    all_gather x1, waiting for transfers between devices, per_device(): lax.all_gather(wide_block, 'dp', axis=0, tiled=True)  134 us
    psum x1, blocking collectives, per_device(): summed = lax.psum(partial_value, 'tensor').astype(jnp.bfloat16)  70 us
    all_to_all x1, blocking collectives, per_device(): lax.all_to_all(train_logs, 'tensor', split_axis=0, concat_axis=1, tiled=T...  34 us
    all_gather x1, blocking collectives, per_device(): wide_block = lax.all_gather(query_block, 'tensor', axis=1, tiled=True)  27 us
  transfers between devices with their start and end apart: 2, of which 2 were waited for; matrix products, arithmetic and copies ran while one was open for 0% of the time, Pallas kernels for 0%

commit v1 on v0

--- a/solution.py
+++ b/solution.py
@@ -47,7 +47,7 @@
     doc_hot = (doc_ids[:, None] == doc_labels[None, :]).astype(jnp.float32)
     doc_part = jnp.dot(scores, doc_hot, precision=lax.Precision.HIGHEST)
     total_rows = local_rows * lax.axis_size("tensor") * lax.axis_size("dp")
-    doc_total = lax.psum(doc_part, ("dp", "tensor"))
+    doc_total = lax.psum(lax.psum(doc_part, "tensor"), "dp")
     doc_influence = doc_total / math.sqrt(total_rows / DOCS)
     return (scores, doc_influence)
 

time: 762 us -> 717 us (0.941)
  waiting for transfers between devices: 600 us -> 555 us
    psum x1 -> x2, waiting for transfers between devices: 466 us -> 422 us  [per_device(): doc_total = lax.psum(lax.psum(doc_part, 'tensor'), 'dp')]
  transfers between devices with their start and end apart: 2 -> 3, of which waited for: 2 -> 3; matrix products, arithmetic and copies ran while one was open for 0% -> 0% of each run, Pallas kernels for 0% -> 0%
where the time goes in v1:
time: 717 us; the launch traced here: 716 us
  waiting for transfers between devices  555 us (77%)
  blocking collectives  131 us (18%)
  between operations  13.9 us (2%)
  matrix products  9.8 us (1%)
    psum x2, waiting for transfers between devices, per_device(): doc_total = lax.psum(lax.psum(doc_part, 'tensor'), 'dp')  422 us
    all_gather x1, waiting for transfers between devices, per_device(): lax.all_gather(wide_block, 'dp', axis=0, tiled=True)  133 us
    psum x1, blocking collectives, per_device(): summed = lax.psum(partial_value, 'tensor').astype(jnp.bfloat16)  70 us
    all_to_all x1, blocking collectives, per_device(): lax.all_to_all(train_logs, 'tensor', split_axis=0, concat_axis=1, tiled=T...  34 us
    all_gather x1, blocking collectives, per_device(): wide_block = lax.all_gather(query_block, 'tensor', axis=1, tiled=True)  27 us
  transfers between devices with their start and end apart: 3, of which 3 were waited for; matrix products, arithmetic and copies ran while one was open for 0% of the time, Pallas kernels for 0%

profile of v1, /device:TPU:2, one launch (start us, length us, event | category | flops | bytes accessed | tf_op | source)
XLA Modules:
  0.0 716.2 jit_solution(8600586204356548174)
XLA Ops:
  7.2 0.0 all-gather.2.cloned.1.call-start
  7.2 0.9 convert_reduce_fusion
  8.1 0.7 fusion.4
  8.8 1.3 fusion.5
  10.1 1.7 fusion.6
  11.8 0.1 pad_maximum_fusion
  11.8 70.0 %all-reduce.7 = bf16[1024,128]{0,1:T(8,128)(2,1)S(1)} all-reduce(f32[1024,128]{0,1:T(8,128)S(1)} %pad_maximum_fusion), channel_id=1, replica_groups=mesh['dp'=32,'tensor'=16] {'tensor'}, use_global_device_ids=true, to_apply=%region_0.0 | all-reduce | flops 131072 | bytes 786432 | tf_op jit(solution)/shard_map/psum | solution.py:27
  81.9 0.1 broadcast_multiply_fusion.1
  82.0 0.1 mul.30
  82.0 0.2 fusion.1
  82.2 0.1 reshape.42
  82.3 0.1 divide_convert_fusion
  82.4 27.0 %all_gather.6 = bf16[24,4096]{1,0:T(8,128)(2,1)} all-gather(bf16[24,256]{1,0:T(8,128)(2,1)S(1)} %divide_convert_fusion), channel_id=1, replica_groups=mesh['dp'=32,'tensor'=16] {'tensor'}, dimensions={1}, use_global_device_ids=true | all-gather | bytes 208896 | tf_op jit(solution)/shard_map/all_gather | solution.py:38
  109.4 0.0 all-gather.2.cloned.1.call-update
  109.4 0.0 all-reduce.4.cloned.1.call-start
  109.4 34.0 %all_to_all.19 = bf16[16,256,256]{2,1,0:T(8,128)(2,1)S(1)} all-to-all(bf16[16,256,256]{2,1,0:T(8,128)(2,1)} %bitcast.15), channel_id=1, replica_groups=mesh['dp'=32,'tensor'=16] {'tensor'}, dimensions={0} | all-to-all | bytes 4194304 | tf_op jit(solution)/shard_map/all_to_all | solution.py:36
  143.5 2.4 copy.12
  145.9 133.4 %all-gather.2.cloned.1.call-done = bf16[768,4096]{1,0:T(8,128)(2,1)} async-done(((bf16[24,4096]{1,0:T(8,128)(2,1)}), bf16[768,4096]{1,0:T(8,128)(2,1)}) %all-gather.2.cloned.1.call-update) | async-done | bytes 6291472 | tf_op jit(solution)/shard_map/all_gather | solution.py:40
  279.2 5.2 convolution_multiply_fusion
  284.5 1.5 fusion
  286.0 0.0 all-reduce.6.cloned.1.call-start
  286.0 148.7 %all-reduce.4.cloned.1.call-done = f32[768,256]{1,0:T(8,128)} async-done(((f32[768,256]{1,0:T(8,128)}), f32[768,256]{1,0:T(8,128)}) %all-reduce.4.cloned.1.call-update) | async-done | bytes 786448 | tf_op jit(solution)/shard_map/psum | solution.py:50
  434.8 272.8 %all-reduce.6.cloned.1.call-done = f32[768,256]{1,0:T(8,128)} async-done(((f32[768,256]{1,0:T(8,128)}), f32[768,256]{1,0:T(8,128)}) %all-reduce.6.cloned.1.call-update) | async-done | bytes 786448 | tf_op jit(solution)/shard_map/psum | solution.py:50
  707.6 2.1 broadcast_multiply_fusion
  (10 shorter events, 0.1 us)
Async XLA Ops:
  7.2 1.7 copy-start
  7.2 272.1 %all-gather.2.cloned.1.call-start = ((), (), s32[]{:S(2)}) async-start(), calls=%async_computation.1 | async-start | bytes 6488064 | tf_op jit(solution)/shard_map/all_gather | solution.py:40
  109.4 325.4 %all-reduce.4.cloned.1.call-start = ((), (), s32[]{:S(2)}) async-start(), calls=%async_computation.2 | async-start | bytes 1572864 | tf_op jit(solution)/shard_map/psum | solution.py:50
  279.2 5.2 copy-start.2
  284.5 425.2 %copy-start.1 = (f32[768,256]{1,0:T(8,128)}, f32[768,256]{1,0:T(8,128)S(1)}, u32[]{:S(2)}) copy-start(f32[768,256]{1,0:T(8,128)S(1)} %convolution_multiply_fusion) | copy-start | bytes 2359300
  286.0 421.6 %all-reduce.6.cloned.1.call-start = ((), (), s32[]{:S(2)}) async-start(), calls=%async_computation.3 | async-start | bytes 1572864 | tf_op jit(solution)/shard_map/psum | solution.py:50
Sparse Core Ops, SparseCore 0:
  109.5 169.6 all-gather.1
  286.1 148.6 all-reduce.3
  437.9 269.6 all-reduce.5
